TPU v7x, 32 devices: a whole 2x2x4 slice. The times are simulated.
32 devices in a mesh: loop: 8 (over y, x, core), dp: 4 (over z).
Axes of the slice: x: 2, y: 2, z: 4, core: 2. Of those that a mesh axis runs over, the one named last changes fastest.
Arguments:
- codes: bfloat16 [2048, 16, 1024], P(('loop', 'dp')), may hold values from -64 to 64, as said below
- cand_hidden: bfloat16 [2048, 1024], P(('loop', 'dp')), may hold values from -5 to 5, as said below
- proj: bfloat16 [1024, 1024], replicated, may hold values from -1 to 2, as said below
- gold: int32 [2048], P(('loop', 'dp')), may hold values from 0 to 511
Outputs:
- context_loss: float32 [2048], P(('loop', 'dp'))
- code_grad: float32 [2048, 16, 1024], P(('loop', 'dp'))
- proj_grad: float32 [1024, 1024], P(('loop', 'dp'))
Inputs may be any that keep to these rules, and one draw needn't show every extreme that they name: codes stay within this range. `cand_hidden`: CLS states stay within this range. `proj`: projection entries stay within this range.
All inputs are finite; a program needn't handle non-finite values.
Results may differ from a plain program's by a relative error of at most 0.0085.
Values may be sent and summed in bfloat16 or wider, within the bound.
A program may use at most 128 MiB of HBM per device.

v0:
```python
import jax
import jax.numpy as jnp
from jax import lax
from jax.sharding import PartitionSpec as P


def block_logits(cand_embed, code_rows, ctx_rows, inv_scale):
    raw = lax.dot_general(
        cand_embed, code_rows, (((1,), (1,)), ((), ())), preferred_element_type=jnp.float32
    )
    return raw.reshape(cand_embed.shape[0], ctx_rows, -1) * inv_scale


def code_softmax(logits):
    top_logit = jnp.max(logits, axis=-1, keepdims=True)
    weights = jnp.exp(logits - top_logit)
    probs = weights / jnp.sum(weights, axis=-1, keepdims=True)
    scores = jnp.sum(probs * logits, axis=-1)
    return (probs, scores)


def score_block(cand_embed, code_rows, ctx_rows, inv_scale):
    logits = block_logits(cand_embed, code_rows, ctx_rows, inv_scale)
    probs, scores = code_softmax(logits)
    return (logits, probs, scores)


def logit_grads(logits, probs, scores, score_grad, inv_scale):
    values = score_grad[:, :, None] * probs * (1.0 + logits - scores[:, :, None]) * inv_scale
    return values.astype(jnp.bfloat16).reshape(logits.shape[0], -1)


def local(codes, cand_hidden, proj, gold):
    ctx_rows, codes_per, model_width = codes.shape
    inv_scale = model_width ** (-0.5)
    code_rows = codes.reshape(ctx_rows * codes_per, model_width)
    cand_embed = jnp.dot(cand_hidden, proj, preferred_element_type=jnp.float32).astype(jnp.bfloat16)
    everyone = lax.all_gather(cand_embed, "loop", axis=0, tiled=True)
    logits, probs, scores = score_block(everyone, code_rows, ctx_rows, inv_scale)
    top_score = jnp.max(scores, axis=0)
    log_total = top_score + jnp.log(jnp.sum(jnp.exp(scores - top_score[None, :]), axis=0))
    cand_ids = jnp.arange(everyone.shape[0], dtype=jnp.int32)
    gold_hot = (cand_ids[:, None] == gold[None, :]).astype(jnp.float32)
    context_loss = log_total - jnp.sum(gold_hot * scores, axis=0)
    score_grad = jnp.exp(scores - log_total[None, :]) - gold_hot
    grads = logit_grads(logits, probs, scores, score_grad, inv_scale)
    code_grad = lax.dot_general(
        grads, everyone, (((0,), (0,)), ((), ())), preferred_element_type=jnp.float32
    )
    embed_grad = lax.psum_scatter(
        jnp.dot(grads, code_rows, preferred_element_type=jnp.float32),
        "loop",
        scatter_dimension=0,
        tiled=True,
    )
    embed_low = embed_grad.astype(jnp.bfloat16)
    proj_grad = lax.psum_scatter(
        lax.dot_general(
            cand_hidden, embed_low, (((0,), (0,)), ((), ())), preferred_element_type=jnp.float32
        ),
        ("loop", "dp"),
        scatter_dimension=0,
        tiled=True,
    )
    return (context_loss, code_grad.reshape(ctx_rows, codes_per, model_width), proj_grad)


def solution(mesh):
    return jax.shard_map(
        local,
        mesh=mesh,
        in_specs=(P(("loop", "dp"), None, None), P(("loop", "dp"), None), P(), P(("loop", "dp"))),
        out_specs=(P(("loop", "dp")), P(("loop", "dp"), None, None), P(("loop", "dp"), None)),
        check_vma=False,
    )
```

profile of v0, /device:TPU:0, one launch (start us, length us, event | category | flops | bytes accessed | tf_op | source)
XLA Modules:
  0.0 254.9 jit_solution(8407832722364254355)
XLA Ops:
  7.2 0.0 copy-start
  7.2 0.0 all-gather.2.cloned.1.call-start
  7.2 2.9 %convolution_convert_fusion = bf16[64,1024]{1,0:T(8,128)(2,1)} fusion(bf16[64,1024]{1,0:T(8,128)(2,1)} %param.5, bf16[1024,1024]{1,0:T(8,128)(2,1)} %param.6), kind=kOutput, calls=%fused_computation.12 | convolution fusion | flops 134283264 | bytes 2359296 | tf_op jit(solution)/shard_map/dot_general | solution.py:37
  10.2 0.0 all-gather.2.cloned.1.call-update
  10.2 0.0 reduce-scatter.5.cloned.1.call-start
  10.2 26.3 %all-gather.2.cloned.1.call-done = bf16[512,1024]{1,0:T(8,128)(2,1)} async-done(((bf16[64,1024]{1,0:T(8,128)(2,1)}), bf16[512,1024]{1,0:T(8,128)(2,1)}) %all-gather.2.cloned.1.call-update) | async-done | bytes 1048592 | tf_op jit(solution)/shard_map/all_gather | solution.py:38
  36.6 2.7 %multiply_reduce_fusion.1 = (f32[512,64]{0,1:T(8,128)S(1)}, f32[512,64,16]{0,1,2:T(8,128)S(1)}) fusion(bf16[64,16,1024]{2,1,0:T(8,128)(2,1)S(1)} %copy-done, bf16[512,1024]{1,0:T(8,128)(2,1)} %all-gather.2.cloned.1.call-done), kind=kOutput, calls=%fused_computation.10 | convolution fusion | flops 1074757632 | bytes 5373952 | tf_op jit(solution)/shard_map/dot_general | solution.py:8
  39.3 0.3 fusion.1
  39.7 0.9 copy-done.1
  40.6 0.5 multiply_reduce_fusion
  41.1 0.1 reduce_max.19
  41.2 0.2 select_reduce_fusion
  41.4 0.5 fusion.15
  42.0 0.1 convert_subtract_fusion
  42.1 2.3 multiply_convert_fusion
  44.4 4.2 %fusion.6 = f32[512,1024]{1,0:T(8,128)} fusion(bf16[512,64,16]{0,1,2:T(8,128)(2,1)S(1)} %multiply_convert_fusion, bf16[64,16,1024]{2,1,0:T(8,128)(2,1)S(1)} %copy-done), kind=kOutput, calls=%fused_computation.11 | convolution fusion | flops 1073741824 | bytes 5242880 | tf_op jit(solution)/shard_map/dot_general | solution.py:51
  48.6 0.0 reduce-scatter.5.cloned.1.call-update
  48.6 0.0 reduce-scatter.7.cloned.1.call-start
  48.7 41.2 %reduce-scatter.5.cloned.1.call-done = f32[64,1024]{1,0:T(8,128)} async-done(((f32[512,1024]{1,0:T(8,128)}), f32[64,1024]{1,0:T(8,128)}) %reduce-scatter.5.cloned.1.call-update) | async-done | bytes 262160 | tf_op jit(solution)/shard_map/reduce_scatter | solution.py:50
  89.9 3.7 %convolution_bitcast_fusion = f32[1024,1024]{0,1:T(8,128)} fusion(bf16[64,1024]{1,0:T(8,128)(2,1)S(1)} %copy-done.2, f32[64,1024]{1,0:T(8,128)} %reduce-scatter.5.cloned.1.call-done), kind=kOutput, calls=%fused_computation | convolution fusion | flops 134283264 | bytes 4587520 | tf_op jit(solution)/shard_map/dot_general | solution.py:58
  93.6 5.3 %copy.16 = f32[1024,1024]{1,0:T(8,128)} copy(f32[1024,1024]{0,1:T(8,128)} %convolution_bitcast_fusion) | data formatting | bytes 8388608
  99.0 0.0 reduce-scatter.7.cloned.1.call-update
  99.0 4.7 %fusion.9 = f32[64,16,1024]{2,1,0:T(8,128)} fusion(bf16[512,1024]{1,0:T(8,128)(2,1)} %all-gather.2.cloned.1.call-done, bf16[512,64,16]{0,1,2:T(8,128)(2,1)S(1)} %multiply_convert_fusion), kind=kOutput, calls=%fused_computation.13 | convolution fusion | flops 1073741824 | bytes 6291456 | tf_op jit(solution)/shard_map/dot_general | solution.py:47
  103.6 144.7 %reduce-scatter.7.cloned.1.call-done = f32[32,1024]{1,0:T(8,128)} async-done(((f32[1024,1024]{1,0:T(8,128)}), f32[32,1024]{1,0:T(8,128)}) %reduce-scatter.7.cloned.1.call-update) | async-done | bytes 131088
  (6 shorter events, 0.0 us)
Async XLA Ops:
  7.2 29.4 %copy-start = (bf16[64,16,1024]{2,1,0:T(8,128)(2,1)S(1)}, bf16[64,16,1024]{2,1,0:T(8,128)(2,1)}, u32[]{:S(2)}) copy-start(bf16[64,16,1024]{2,1,0:T(8,128)(2,1)} %param.4) | copy-start | bytes 6291460
  7.2 29.4 %all-gather.2.cloned.1.call-start = ((), (), s32[]{:S(2)}) async-start(), calls=%async_computation.2 | async-start | bytes 1179648 | tf_op jit(solution)/shard_map/all_gather | solution.py:38
  10.2 79.7 %reduce-scatter.5.cloned.1.call-start = ((), (), s32[]{:S(2)}) async-start(), calls=%async_computation.3 | async-start | bytes 2359296 | tf_op jit(solution)/shard_map/reduce_scatter | solution.py:50
  39.3 1.3 copy-start.1
  39.3 1.9 copy-start.3
  48.6 41.3 %copy-start.2 = (bf16[64,1024]{1,0:T(8,128)(2,1)S(1)}, bf16[64,1024]{1,0:T(8,128)(2,1)}, u32[]{:S(2)}) copy-start(bf16[64,1024]{1,0:T(8,128)(2,1)} %param.5) | copy-start | bytes 393220
  48.6 199.7 %reduce-scatter.7.cloned.1.call-start = ((), (), s32[]{:S(2)}) async-start(), calls=%async_computation.4 | async-start | bytes 4325376
Sparse Core Ops, SparseCore 0:
  10.4 26.0 all-gather.1
  48.8 41.1 reduce-scatter.4
  99.1 149.1 reduce-scatter.6
where the time goes:
time: 255 us
  waiting for transfers between devices  212 us (83%)
  matrix products  18.2 us (7%)
  between operations  13.8 us (5%)
  local copies, waits for them, and re-layouts  6.32 us (2%)
  other arithmetic  4.1 us (2%)
    unnamed x4, waiting for transfers between devices  145 us
    reduce_scatter x1, waiting for transfers between devices, local(): lax.psum_scatter(jnp.dot(grads, code_rows, preferred_element_type=jnp.flo...  41.2 us
    all_gather x1, waiting for transfers between devices, local(): everyone = lax.all_gather(cand_embed, 'loop', axis=0, tiled=True)  26.3 us
    unnamed x9, local copies, waits for them, and re-layouts  6.32 us
  transfers between devices with their start and end apart: 3, of which 3 were waited for; matrix products, arithmetic and copies ran while one was open for 2% of the time, Pallas kernels for 0%

commit v1 on v0

v1 whole, which is shorter than its diff:
```python
import functools

import jax
import jax.numpy as jnp
from jax import lax
from jax.experimental import pallas as pl
from jax.experimental.pallas import tpu as pltpu
from jax.sharding import PartitionSpec as P

MESH = pl.DeviceIdType.MESH
F32 = jnp.float32
BF16 = jnp.bfloat16
LANES = 128
NT = (((1,), (1,)), ((), ()))


def dot(a, b):
    return jnp.dot(a, b, preferred_element_type=F32)


def body(
    ring, groups, ctx, per,
    codes_ref, hidden_ref, proj_ref, gold_ref,
    loss_ref, gradt_ref, embed_ref, out_ref,
    codes, proj, perm, permt, rows, held, logits, scores, grads, hidt,
    e_own, e_sib, e_sum, e_in, p_own, p_in, q_own, q_in,
    local_sem, h_send, h_recv, hs_send, hs_recv, es_send, es_recv,
    ef_send, ef_recv, z_send, z_recv, q_send, q_recv,
):
    width = hidden_ref.shape[1]
    batch = hidden_ref.shape[0]
    chips = ring // 2
    half = chips * batch
    n_rows = ctx * per
    me = lax.axis_index("loop")
    group = lax.axis_index("dp")
    chip, par = me // 2, me % 2
    sibling = chip * 2 + 1 - par
    inv_scale = width ** -0.5

    get_codes = pltpu.make_async_copy(codes_ref, codes, local_sem.at[0])
    get_proj = pltpu.make_async_copy(proj_ref, proj, local_sem.at[1])
    get_hidden = pltpu.make_async_copy(hidden_ref, held.at[par, chip], local_sem.at[2])
    get_hidden.start()
    get_codes.start()
    get_proj.start()

    barrier = pltpu.get_barrier_semaphore()
    for k in range(1, ring):
        pl.semaphore_signal(barrier, 1, device_id={"loop": (me + k) % ring}, device_id_type=MESH)
    for k in range(1, groups):
        pl.semaphore_signal(barrier, 1, device_id={"dp": (group + k) % groups}, device_id_type=MESH)
    get_hidden.wait()
    pl.semaphore_wait(barrier, ring + groups - 2)

    def send(src, dst, ssem, rsem, where):
        copy = pltpu.make_async_remote_copy(
            src_ref=src, dst_ref=dst, send_sem=ssem, recv_sem=rsem,
            device_id=where, device_id_type=MESH)
        copy.start()
        return copy

    pending = []
    far = []
    for k in range(chips - 1):
        to = (chip + 1 + k) % chips
        far.append(send(hidden_ref, held.at[par, chip], h_send.at[k], h_recv.at[k],
                        {"loop": to * 2 + par}))
    near = [send(hidden_ref, held.at[par, chip], hs_send.at[chips - 1], hs_recv.at[chips - 1],
                 {"loop": sibling})]

    row_tile = 128

    @pl.loop(0, n_rows // row_tile)
    def _(t):
        start = pl.multiple_of(t * row_tile, row_tile)
        r = lax.broadcasted_iota(jnp.int32, (row_tile, n_rows), 0) + start
        c = lax.broadcasted_iota(jnp.int32, (row_tile, n_rows), 1)
        perm[pl.ds(start, row_tile), :] = jnp.where(
            c == (r % ctx) * per + r // ctx, 1.0, 0.0).astype(BF16)
        permt[pl.ds(start, row_tile), :] = jnp.where(
            c == (r % per) * ctx + r // per, 1.0, 0.0).astype(BF16)

    get_codes.wait()
    tile = 256

    @pl.loop(0, width // tile)
    def _(t):
        cols = pl.ds(pl.multiple_of(t * tile, tile), tile)
        rows[:, cols] = dot(perm[...], codes[:, cols]).astype(BF16)

    get_proj.wait()
    for k in range(chips - 1):
        far[k].wait_recv()
        src = (chip + chips - 1 - k) % chips
        near.append(send(held.at[par, src], held.at[par, src], hs_send.at[k], hs_recv.at[k],
                         {"loop": sibling}))

    def forward(h):
        mine = pl.ds(pl.multiple_of(h * half, half), half)

        @pl.loop(0, width // tile)
        def _(t):
            cols = pl.ds(pl.multiple_of(t * tile, tile), tile)
            embed_ref[mine, cols] = dot(
                held[h].reshape(half, width), proj[:, cols]).astype(BF16)

        @pl.loop(0, n_rows // tile)
        def _(t):
            cols = pl.ds(pl.multiple_of(t * tile, tile), tile)
            logits[mine, cols] = lax.dot_general(
                embed_ref[mine, :], rows[cols, :], NT,
                preferred_element_type=F32) * inv_scale

        step = 16

        @pl.loop(0, half // step)
        def _(t):
            at = pl.ds(pl.multiple_of(h * half + t * step, step), step)
            parts = [logits[at, j * LANES:(j + 1) * LANES] for j in range(n_rows // LANES)]
            fold = LANES // ctx

            def across(values, op):
                total = functools.reduce(op, values)
                shift = ctx
                while shift < LANES:
                    total = op(total, pltpu.roll(total, shift, axis=1))
                    shift *= 2
                return total

            top = across(parts, jnp.maximum)
            weights = [jnp.exp(x - top) for x in parts]
            inv = 1.0 / across(weights, jnp.add)
            score = across([w * x for w, x in zip(weights, parts)], jnp.add) * inv
            scores[at, :] = score
            for j, (w, x) in enumerate(zip(weights, parts)):
                logits[at, j * LANES:(j + 1) * LANES] = (w * inv) * (1.0 + x - score) * inv_scale

    forward(par)
    for copy in near:
        copy.wait_recv()
    forward(1 - par)

    all_scores = scores[...]
    top_score = jnp.max(all_scores, axis=0, keepdims=True)
    log_total = top_score + jnp.log(jnp.sum(jnp.exp(all_scores - top_score), axis=0, keepdims=True))
    gold = jnp.concatenate([gold_ref[...]] * (LANES // ctx), axis=1)

    def block(b, picked):
        side, c = b // chips, b % chips
        owner = c * 2 + side
        at = pl.ds(pl.multiple_of(b * batch, batch), batch)
        ids = lax.broadcasted_iota(jnp.int32, (batch, LANES), 0) + owner * batch
        hot = jnp.where(ids == gold, 1.0, 0.0)
        score = scores[at, :]
        score_grad = jnp.exp(score - log_total) - hot
        for j in range(n_rows // LANES):
            lanes = slice(j * LANES, (j + 1) * LANES)
            grads[at, lanes] = (score_grad * logits[at, lanes]).astype(BF16)
        return picked + jnp.sum(hot * score, axis=0, keepdims=True)

    picked = lax.fori_loop(0, ring, block, jnp.zeros((1, LANES), F32))
    loss_ref[...] = (log_total - picked)[:, :ctx]

    chunk = width // ring
    sib = []
    for k in range(chips):
        to = (chip + 1 + k) % chips
        cols = pl.ds(pl.multiple_of(to * 2 * chunk, 2 * chunk), 2 * chunk)
        part = dot(grads[...], rows[:, cols]).astype(BF16)
        e_own[k, 0] = part[:, :chunk]
        e_own[k, 1] = part[:, chunk:]
        sib.append(send(e_own.at[k, 1 - par], e_sib.at[k], es_send.at[k], es_recv.at[k],
                        {"loop": sibling}))
    e_far = []
    for k in range(chips):
        to = (chip + 1 + k) % chips
        sib[k].wait_recv()
        total = e_own[k, par].astype(F32) + e_sib[k].astype(F32)
        e_sum[k] = total.astype(BF16)
        if k < chips - 1:
            e_far.append(send(e_sum.at[k], e_in.at[k], ef_send.at[k], ef_recv.at[k],
                              {"loop": to * 2 + par}))

    @pl.loop(0, (2 * half) // tile)
    def _(t):
        cols = pl.ds(pl.multiple_of(t * tile, tile), tile)
        gradt_ref[:, cols] = lax.dot_general(
            permt[...], grads[cols, :], NT, preferred_element_type=F32).astype(BF16)

    hid_all = held.reshape(2 * half, width)

    @pl.loop(0, width // LANES)
    def _(t):
        cols = pl.ds(pl.multiple_of(t * LANES, LANES), LANES)
        hidt[cols, :] = hid_all[:, cols].T

    total = e_sum[chips - 1].astype(F32)
    for k in range(chips - 1):
        e_far[k].wait_recv()
        total = total + e_in[k].astype(F32)
    p_part = dot(hidt[...], total.astype(BF16))
    out_rows = out_ref.shape[0]
    for g in range(groups):
        for l in range(ring):
            first = (l * groups + g) * out_rows
            p_own[g, l] = p_part[first:first + out_rows].astype(BF16)
    z_far = []
    for k in range(groups - 1):
        to = (group + 1 + k) % groups
        z_far.append(send(p_own.at[to], p_in.at[k], z_send.at[k], z_recv.at[k], {"dp": to}))
    total = p_own[group].astype(F32)
    for k in range(groups - 1):
        z_far[k].wait_recv()
        total = total + p_in[k].astype(F32)
    q_own[...] = total.astype(BF16)
    q_far = []
    for k in range(ring - 1):
        to = (me + 1 + k) % ring
        q_far.append(send(q_own.at[to], q_in.at[me], q_send.at[k], q_recv.at[k], {"loop": to}))
    q_in[me] = q_own[me]
    for k in range(ring - 1):
        q_far[k].wait_recv()
    for l in range(ring):
        out_ref[:, l * chunk:(l + 1) * chunk] = q_in[l].astype(F32)
    for copy in far + near + sib + e_far + z_far + q_far:
        copy.wait_send()


def code_body(gradt_ref, embed_ref, out_ref):
    out_ref[...] = dot(gradt_ref[...], embed_ref[...])


def local(ring, groups, codes, cand_hidden, proj, gold):
    ctx, per, width = codes.shape
    batch = cand_hidden.shape[0]
    n_rows = ctx * per
    chips = ring // 2
    cands = ring * batch
    out_rows = width // (ring * groups)
    chunk = width // ring
    vmem = pl.BlockSpec(memory_space=pltpu.VMEM)
    anywhere = pl.BlockSpec(memory_space=pl.ANY)
    dma = pltpu.SemaphoreType.DMA
    loss, gradt, embed, proj_grad = pl.pallas_call(
        functools.partial(body, ring, groups, ctx, per),
        name="link_step",
        out_shape=(
            jax.ShapeDtypeStruct((1, ctx), F32),
            jax.ShapeDtypeStruct((n_rows, cands), BF16),
            jax.ShapeDtypeStruct((cands, width), BF16),
            jax.ShapeDtypeStruct((out_rows, width), F32),
        ),
        in_specs=[anywhere, vmem, anywhere, vmem],
        out_specs=(vmem, vmem, vmem, vmem),
        scratch_shapes=[
            pltpu.VMEM((n_rows, width), BF16),
            pltpu.VMEM((width, width), BF16),
            pltpu.VMEM((n_rows, n_rows), BF16),
            pltpu.VMEM((n_rows, n_rows), BF16),
            pltpu.VMEM((n_rows, width), BF16),
            pltpu.VMEM((2, chips, batch, width), BF16),
            pltpu.VMEM((cands, n_rows), F32),
            pltpu.VMEM((cands, LANES), F32),
            pltpu.VMEM((cands, n_rows), BF16),
            pltpu.VMEM((width, cands), BF16),
            pltpu.VMEM((chips, 2, cands, chunk), BF16),
            pltpu.VMEM((chips, cands, chunk), BF16),
            pltpu.VMEM((chips, cands, chunk), BF16),
            pltpu.VMEM((chips - 1, cands, chunk), BF16),
            pltpu.VMEM((groups, ring, out_rows, chunk), BF16),
            pltpu.VMEM((groups - 1, ring, out_rows, chunk), BF16),
            pltpu.VMEM((ring, out_rows, chunk), BF16),
            pltpu.VMEM((ring, out_rows, chunk), BF16),
            dma((3,)),
            dma((chips - 1,)), dma((chips - 1,)),
            dma((chips,)), dma((chips,)),
            dma((chips,)), dma((chips,)),
            dma((chips - 1,)), dma((chips - 1,)),
            dma((groups - 1,)), dma((groups - 1,)),
            dma((ring - 1,)), dma((ring - 1,)),
        ],
        compiler_params=pltpu.CompilerParams(
            collective_id=0, has_side_effects=True, vmem_limit_bytes=56 * 2**20),
    )(codes.reshape(n_rows, width), cand_hidden, proj, gold.reshape(1, ctx))
    tiles = 4
    code_grad = pl.pallas_call(
        code_body,
        name="code_grad",
        grid=(tiles,),
        out_shape=jax.ShapeDtypeStruct((n_rows, width), F32),
        in_specs=[
            pl.BlockSpec((n_rows // tiles, cands), lambda t: (t, 0)),
            pl.BlockSpec((cands, width), lambda t: (0, 0)),
        ],
        out_specs=pl.BlockSpec((n_rows // tiles, width), lambda t: (t, 0)),
    )(gradt, embed)
    return loss.reshape(ctx), code_grad.reshape(ctx, per, width), proj_grad


def solution(mesh):
    return jax.shard_map(
        functools.partial(local, mesh.shape["loop"], mesh.shape["dp"]),
        mesh=mesh,
        in_specs=(P(("loop", "dp"), None, None), P(("loop", "dp"), None), P(), P(("loop", "dp"))),
        out_specs=(P(("loop", "dp")), P(("loop", "dp"), None, None), P(("loop", "dp"), None)),
        check_vma=False,
    )
```

time: 255 us -> 54.8 us (0.21)
  waiting for transfers between devices: 212 us -> 0 us
  Pallas kernels: 0 us -> 52.8 us
  matrix products: 18.2 us -> 0 us
  between operations: 13.8 us -> 0.66 us
  local copies, waits for them, and re-layouts: 6.32 us -> 1.18 us
  other arithmetic: 4.1 us -> 0 us
    unnamed x4 -> x0, waiting for transfers between devices: 145 us -> none
    pallas_call x0 -> x2, Pallas kernels: none -> 52.8 us  [the longest x1 47.6 us: local(): pl.pallas_call(functools.partial(body, ring, groups, ctx, per), name='lin...]
    reduce_scatter x1 -> x0, waiting for transfers between devices: 41.2 us -> none  [local(): lax.psum_scatter(jnp.dot(grads, code_rows, preferred_element_type=jnp.flo...]
    all_gather x1 -> x0, waiting for transfers between devices: 26.3 us -> none  [local(): everyone = lax.all_gather(cand_embed, 'loop', axis=0, tiled=True)]
    dot_general x5 -> x0, matrix products: 18.2 us -> none  [the longest x1 4.65 us: local(): lax.dot_general(grads, everyone, (((0,), (0,)), ((), ())), preferred_elem...]
    unnamed x9 -> x6, local copies, waits for them, and re-layouts: 6.32 us -> 1.18 us
  transfers between devices with their start and end apart: 3 -> 0, of which waited for: 3 -> 0; matrix products, arithmetic and copies ran while one was open for 2% -> 0% of each run, Pallas kernels for 0% -> 0%
where the time goes in v1:
time: 54.8 us; the launch traced here: 54.6 us
  Pallas kernels  52.8 us (96%)
  local copies, waits for them, and re-layouts  1.18 us (2%)
  between operations  0.66 us (1%)
    pallas_call x1, Pallas kernels, local(): pl.pallas_call(functools.partial(body, ring, groups, ctx, per), name='lin...  47.6 us
    pallas_call x1, Pallas kernels, local(): pl.pallas_call(code_body, name='code_grad', grid=(tiles,), out_shape=jax....  5.14 us
    unnamed x6, local copies, waits for them, and re-layouts  1.18 us

profile of v1, /device:TPU:0, one launch (start us, length us, event | category | flops | bytes accessed | tf_op | source)
XLA Modules:
  0.0 54.6 jit_solution(1830498626672445217)
XLA Ops:
  0.6 47.6 %link_step.1 = (f32[1,64]{1,0:T(1,128)}, bf16[1024,512]{1,0:T(8,128)(2,1)}, bf16[512,1024]{1,0:T(8,128)(2,1)}, f32[32,1024]{1,0:T(8,128)}) custom-call(bf16[1024,1024]{1,0:T(8,128)(2,1)} %bitcast.5, bf16[64,1024]{1,0:T(8,128)(2,1)} %hidden_ref.1, bf16[1024,1024]{1,0:T(8,128)(2,1)} %proj_ref.1, s32[1,64]{1,0:T(1,128)} %bitcast.6), custom_call_target="tpu_custom_call" | custom-call | tf_op jit(solution)/shard_map/link_step/pallas_call | solution.py:245
  48.3 0.0 copy-start.1
  48.3 0.0 copy-start
  48.3 5.1 %code_grad.1 = f32[1024,1024]{1,0:T(8,128)} custom-call(bf16[1024,512]{1,0:T(8,128)(2,1)} %get-tuple-element.8.gradt_ref, bf16[512,1024]{1,0:T(8,128)(2,1)} %get-tuple-element.9.embed_ref), custom_call_target="tpu_custom_call" | custom-call | tf_op jit(solution)/shard_map/code_grad/pallas_call | solution.py:287
  53.4 0.0 copy-done.1
  53.4 0.5 copy.9
  53.9 0.0 copy-done
  53.9 0.7 %copy.10 = f32[32,1024]{1,0:T(8,128)} copy(f32[32,1024]{1,0:T(8,128)S(1)} %copy-done) | data formatting | bytes 262144
Async XLA Ops:
  48.3 5.2 %copy-start.1 = (f32[1,64]{1,0:T(1,128)S(1)}, f32[1,64]{1,0:T(1,128)}, u32[]{:S(2)}) copy-start(f32[1,64]{1,0:T(1,128)} %get-tuple-element.7) | copy-start | bytes 772
  48.3 5.7 %copy-start = (f32[32,1024]{1,0:T(8,128)S(1)}, f32[32,1024]{1,0:T(8,128)}, u32[]{:S(2)}) copy-start(f32[32,1024]{1,0:T(8,128)} %get-tuple-element.16) | copy-start | bytes 393220

commit v2 on v1

v2 whole, which is shorter than its diff:
```python
import functools

import jax
import jax.numpy as jnp
from jax import lax
from jax.experimental import pallas as pl
from jax.experimental.pallas import tpu as pltpu
from jax.sharding import PartitionSpec as P

MESH = pl.DeviceIdType.MESH
F32 = jnp.float32
BF16 = jnp.bfloat16
LANES = 128
STEP = 32
LAG = 1
NT = (((1,), (1,)), ((), ()))


def dot(a, b):
    return jnp.dot(a, b, preferred_element_type=F32)


def body(
    ring, groups, ctx, per,
    codes_ref, hidden_ref, proj_ref, gold_ref,
    loss_ref, gradt_ref, embed_ref, q_in,
    codes, proj, perm, rows, held, embed, logits, slopes, scores, grads, gradt, hidt,
    e_own, e_sib, e_sum, e_in, p_own, p_in, q_own,
    local_sem, h_send, h_recv, hs_send, hs_recv, es_send, es_recv,
    ef_send, ef_recv, z_send, z_recv, q_send, q_recv,
):
    width = hidden_ref.shape[1]
    batch = hidden_ref.shape[0]
    chips = ring // 2
    half = chips * batch
    n_rows = ctx * per
    me = lax.axis_index("loop")
    group = lax.axis_index("dp")
    chip, par = me // 2, me % 2
    sibling = chip * 2 + 1 - par
    inv_scale = width ** -0.5

    get_codes = pltpu.make_async_copy(codes_ref, codes, local_sem.at[0])
    get_proj = pltpu.make_async_copy(proj_ref, proj, local_sem.at[1])
    get_hidden = pltpu.make_async_copy(hidden_ref, held.at[me], local_sem.at[2])
    get_hidden.start()
    get_codes.start()
    get_proj.start()

    barrier = pltpu.get_barrier_semaphore()
    for k in range(1, ring):
        pl.semaphore_signal(barrier, 1, device_id={"loop": (me + k) % ring}, device_id_type=MESH)
    for k in range(1, groups):
        pl.semaphore_signal(barrier, 1, device_id={"dp": (group + k) % groups}, device_id_type=MESH)
    row_tile = 128

    @pl.loop(0, n_rows // row_tile)
    def _(t):
        start = pl.multiple_of(t * row_tile, row_tile)
        r = lax.broadcasted_iota(jnp.int32, (row_tile, n_rows), 0) + start
        c = lax.broadcasted_iota(jnp.int32, (row_tile, n_rows), 1)
        perm[pl.ds(start, row_tile), :] = jnp.where(
            c == (r % ctx) * per + r // ctx, 1.0, 0.0).astype(BF16)

    get_hidden.wait()
    pl.semaphore_wait(barrier, ring + groups - 2)

    def send(src, dst, ssem, rsem, where):
        copy = pltpu.make_async_remote_copy(
            src_ref=src, dst_ref=dst, send_sem=ssem, recv_sem=rsem,
            device_id=where, device_id_type=MESH)
        copy.start()
        return copy

    pending = []
    far = []
    for k in range(chips - 1):
        to = (chip + 1 + k) % chips
        far.append(send(hidden_ref, held.at[me], h_send.at[k], h_recv.at[k],
                        {"loop": to * 2 + par}))
    near = [send(hidden_ref, held.at[me], hs_send.at[chips - 1], hs_recv.at[chips - 1],
                 {"loop": sibling})]

    get_codes.wait()
    tile = 256

    @pl.loop(0, width // tile)
    def _(t):
        cols = pl.ds(pl.multiple_of(t * tile, tile), tile)
        rows[:, cols] = dot(perm[...], codes[:, cols]).astype(BF16)

    get_proj.wait()

    def forward(owners):
        count = len(owners) * batch
        spots = [pl.ds(pl.multiple_of(o * batch, batch), batch) for o in owners]

        @pl.loop(0, width // tile)
        def _(t):
            cols = pl.ds(pl.multiple_of(t * tile, tile), tile)
            part = dot(jnp.concatenate([held[o] for o in owners], axis=0), proj[:, cols])
            for j, spot in enumerate(spots):
                embed[spot, cols] = part[j * batch:(j + 1) * batch].astype(BF16)

        @pl.loop(0, n_rows // tile)
        def _(t):
            cols = pl.ds(pl.multiple_of(t * tile, tile), tile)
            logits[:count, cols] = lax.dot_general(
                jnp.concatenate([embed[spot, :] for spot in spots], axis=0), rows[cols, :], NT,
                preferred_element_type=F32) * inv_scale

        step = STEP
        per_owner = batch // step

        for j, o in enumerate(owners):
            @pl.loop(0, per_owner)
            def _(t):
                src = pl.ds(pl.multiple_of(j * batch + t * step, step), step)
                at = pl.ds(pl.multiple_of(o * batch + t * step, step), step)
                parts = [logits[src, i * LANES:(i + 1) * LANES] for i in range(n_rows // LANES)]

                def across(values, op):
                    while len(values) > 1:
                        values = [op(*values[i:i + 2]) if i + 1 < len(values) else values[i]
                                  for i in range(0, len(values), 2)]
                    total = values[0]
                    shift = ctx
                    while shift < LANES:
                        total = op(total, pltpu.roll(total, shift, axis=1))
                        shift *= 2
                    return total

                top = across(parts, jnp.maximum)
                weights = [jnp.exp(x - top) for x in parts]
                inv = 1.0 / across(weights, jnp.add)
                score = across([w * x for w, x in zip(weights, parts)], jnp.add) * inv
                scores[at, :] = score
                rest = 1.0 - score
                scaled = inv * inv_scale
                for i, (w, x) in enumerate(zip(weights, parts)):
                    slopes[at, i * LANES:(i + 1) * LANES] = (w * scaled) * (x + rest)

    near[0].wait_recv()
    forward([me, sibling])
    mine, theirs = [], []
    for k in range(chips - 1):
        far[k].wait_recv()
        src = (chip + chips - 1 - k) % chips
        near.append(send(held.at[src * 2 + par], held.at[src * 2 + par], hs_send.at[k],
                         hs_recv.at[k], {"loop": sibling}))
        mine.append(src * 2 + par)
        theirs.append(src * 2 + 1 - par)
    forward(mine)
    for copy in near[1:]:
        copy.wait_recv()
    forward(theirs)
    put_embed = pltpu.make_async_copy(embed, embed_ref, local_sem.at[3])
    put_embed.start()

    all_scores = scores[...]
    top_score = jnp.max(all_scores, axis=0, keepdims=True)
    log_total = top_score + jnp.log(jnp.sum(jnp.exp(all_scores - top_score), axis=0, keepdims=True))
    gold = jnp.concatenate([gold_ref[...]] * (LANES // ctx), axis=1)

    def block(b, picked):
        at = pl.ds(pl.multiple_of(b * batch, batch), batch)
        ids = lax.broadcasted_iota(jnp.int32, (batch, LANES), 0) + b * batch
        hot = jnp.where(ids == gold, 1.0, 0.0)
        score = scores[at, :]
        score_grad = jnp.exp(score - log_total) - hot
        for j in range(n_rows // LANES):
            lanes = slice(j * LANES, (j + 1) * LANES)
            grads[at, lanes] = (score_grad * slopes[at, lanes]).astype(BF16)
        return picked + jnp.sum(hot * score, axis=0, keepdims=True)

    picked = lax.fori_loop(0, ring, block, jnp.zeros((1, LANES), F32))
    loss_ref[...] = (log_total - picked)[:, :ctx]

    chunk = width // ring
    sib, e_far = [], []

    def finish(k):
        to = (chip + 1 + k) % chips
        sib[k].wait_recv()
        total = e_own[k, par].astype(F32) + e_sib[k].astype(F32)
        e_sum[k] = total.astype(BF16)
        if k < chips - 1:
            e_far.append(send(e_sum.at[k], e_in.at[k], ef_send.at[k], ef_recv.at[k],
                              {"loop": to * 2 + par}))

    for k in range(chips):
        to = (chip + 1 + k) % chips
        cols = pl.ds(pl.multiple_of(to * 2 * chunk, 2 * chunk), 2 * chunk)
        part = dot(grads[...], rows[:, cols]).astype(BF16)
        e_own[k, 0] = part[:, :chunk]
        e_own[k, 1] = part[:, chunk:]
        sib.append(send(e_own.at[k, 1 - par], e_sib.at[k], es_send.at[k], es_recv.at[k],
                        {"loop": sibling}))
        if k >= LAG:
            finish(k - LAG)
    for k in range(chips - LAG, chips):
        finish(k)

    @pl.loop(0, n_rows // row_tile)
    def _(t):
        start = pl.multiple_of(t * row_tile, row_tile)
        r = lax.broadcasted_iota(jnp.int32, (row_tile, n_rows), 0) + start
        c = lax.broadcasted_iota(jnp.int32, (row_tile, n_rows), 1)
        perm[pl.ds(start, row_tile), :] = jnp.where(
            c == (r % per) * ctx + r // per, 1.0, 0.0).astype(BF16)

    @pl.loop(0, (2 * half) // tile)
    def _(t):
        cols = pl.ds(pl.multiple_of(t * tile, tile), tile)
        gradt[:, cols] = lax.dot_general(
            perm[...], grads[cols, :], NT, preferred_element_type=F32).astype(BF16)

    put_gradt = pltpu.make_async_copy(gradt, gradt_ref, local_sem.at[4])
    put_gradt.start()
    hid_all = held.reshape(2 * half, width)

    @pl.loop(0, width // LANES)
    def _(t):
        cols = pl.ds(pl.multiple_of(t * LANES, LANES), LANES)
        hidt[cols, :] = hid_all[:, cols].T

    total = e_sum[chips - 1].astype(F32)
    for k in range(chips - 1):
        e_far[k].wait_recv()
        total = total + e_in[k].astype(F32)
    p_part = dot(hidt[...], total.astype(BF16))
    out_rows = q_in.shape[1]
    for g in range(groups):
        for l in range(ring):
            first = (l * groups + g) * out_rows
            p_own[g, l] = p_part[first:first + out_rows].astype(BF16)
    z_far = []
    for k in range(groups - 1):
        to = (group + 1 + k) % groups
        z_far.append(send(p_own.at[to], p_in.at[k], z_send.at[k], z_recv.at[k], {"dp": to}))
    total = p_own[group].astype(F32)
    for k in range(groups - 1):
        z_far[k].wait_recv()
        total = total + p_in[k].astype(F32)
    q_own[...] = total.astype(BF16)
    q_far = []
    for k in range(ring - 1):
        to = (me + 1 + k) % ring
        q_far.append(send(q_own.at[to], q_in.at[me], q_send.at[k], q_recv.at[k], {"loop": to}))
    q_in[me] = q_own[me]
    for k in range(ring - 1):
        q_far[k].wait_recv()
    put_embed.wait()
    put_gradt.wait()
    for copy in far + near + sib + e_far + z_far + q_far:
        copy.wait_send()


def code_body(gradt_ref, embed_ref, loss_ref, parts_ref, out_ref, loss_out, proj_out):
    out_ref[...] = dot(gradt_ref[...], embed_ref[...])

    @pl.when(pl.program_id(0) == 0)
    def _():
        chunk = parts_ref.shape[2]
        loss_out[...] = loss_ref[...]
        for l in range(parts_ref.shape[0]):
            proj_out[:, l * chunk:(l + 1) * chunk] = parts_ref[l].astype(F32)


def local(ring, groups, codes, cand_hidden, proj, gold):
    ctx, per, width = codes.shape
    batch = cand_hidden.shape[0]
    n_rows = ctx * per
    chips = ring // 2
    cands = ring * batch
    out_rows = width // (ring * groups)
    chunk = width // ring
    vmem = pl.BlockSpec(memory_space=pltpu.VMEM)
    anywhere = pl.BlockSpec(memory_space=pl.ANY)
    dma = pltpu.SemaphoreType.DMA
    loss, gradt, embed, parts = pl.pallas_call(
        functools.partial(body, ring, groups, ctx, per),
        name="link_step",
        out_shape=(
            jax.ShapeDtypeStruct((1, ctx), F32),
            jax.ShapeDtypeStruct((n_rows, cands), BF16),
            jax.ShapeDtypeStruct((cands, width), BF16),
            jax.ShapeDtypeStruct((ring, out_rows, chunk), BF16),
        ),
        in_specs=[anywhere, vmem, anywhere, vmem],
        out_specs=(vmem, anywhere, anywhere, vmem),
        scratch_shapes=[
            pltpu.VMEM((n_rows, width), BF16),
            pltpu.VMEM((width, width), BF16),
            pltpu.VMEM((n_rows, n_rows), BF16),
            pltpu.VMEM((n_rows, width), BF16),
            pltpu.VMEM((ring, batch, width), BF16),
            pltpu.VMEM((cands, width), BF16),
            pltpu.VMEM((cands, n_rows), F32),
            pltpu.VMEM((cands, n_rows), F32),
            pltpu.VMEM((cands, LANES), F32),
            pltpu.VMEM((cands, n_rows), BF16),
            pltpu.VMEM((n_rows, cands), BF16),
            pltpu.VMEM((width, cands), BF16),
            pltpu.VMEM((chips, 2, cands, chunk), BF16),
            pltpu.VMEM((chips, cands, chunk), BF16),
            pltpu.VMEM((chips, cands, chunk), BF16),
            pltpu.VMEM((chips - 1, cands, chunk), BF16),
            pltpu.VMEM((groups, ring, out_rows, chunk), BF16),
            pltpu.VMEM((groups - 1, ring, out_rows, chunk), BF16),
            pltpu.VMEM((ring, out_rows, chunk), BF16),
            dma((5,)),
            dma((chips - 1,)), dma((chips - 1,)),
            dma((chips,)), dma((chips,)),
            dma((chips,)), dma((chips,)),
            dma((chips - 1,)), dma((chips - 1,)),
            dma((groups - 1,)), dma((groups - 1,)),
            dma((ring - 1,)), dma((ring - 1,)),
        ],
        compiler_params=pltpu.CompilerParams(
            collective_id=0, has_side_effects=True, vmem_limit_bytes=56 * 2**20),
    )(codes.reshape(n_rows, width), cand_hidden, proj, gold.reshape(1, ctx))
    tiles = 4
    code_grad, loss, proj_grad = pl.pallas_call(
        code_body,
        name="code_grad",
        grid=(tiles,),
        out_shape=(
            jax.ShapeDtypeStruct((n_rows, width), F32),
            jax.ShapeDtypeStruct((1, ctx), F32),
            jax.ShapeDtypeStruct((out_rows, width), F32),
        ),
        in_specs=[
            pl.BlockSpec((n_rows // tiles, cands), lambda t: (t, 0)),
            pl.BlockSpec((cands, width), lambda t: (0, 0)),
            pl.BlockSpec((1, ctx), lambda t: (0, 0)),
            pl.BlockSpec((ring, out_rows, chunk), lambda t: (0, 0, 0)),
        ],
        out_specs=(
            pl.BlockSpec((n_rows // tiles, width), lambda t: (t, 0)),
            pl.BlockSpec((1, ctx), lambda t: (0, 0)),
            pl.BlockSpec((out_rows, width), lambda t: (0, 0)),
        ),
    )(gradt, embed, loss, parts)
    return loss.reshape(ctx), code_grad.reshape(ctx, per, width), proj_grad


def solution(mesh):
    return jax.shard_map(
        functools.partial(local, mesh.shape["loop"], mesh.shape["dp"]),
        mesh=mesh,
        in_specs=(P(("loop", "dp"), None, None), P(("loop", "dp"), None), P(), P(("loop", "dp"))),
        out_specs=(P(("loop", "dp")), P(("loop", "dp"), None, None), P(("loop", "dp"), None)),
        check_vma=False,
    )
```

time: 54.8 us -> 49.7 us (0.907)
  Pallas kernels: 52.8 us -> 48.9 us
  local copies, waits for them, and re-layouts: 1.18 us -> 0 us
    pallas_call x1, Pallas kernels: 47.6 us -> 43.7 us  [local(): pl.pallas_call(functools.partial(body, ring, groups, ctx, per), name='lin...]
    unnamed x6 -> x0, local copies, waits for them, and re-layouts: 1.18 us -> none
where the time goes in v2:
time: 49.7 us; the launch traced here: 49.5 us
  Pallas kernels  48.9 us (98%)
  between operations  0.64 us (1%)
    pallas_call x1, Pallas kernels, local(): pl.pallas_call(functools.partial(body, ring, groups, ctx, per), name='lin...  43.7 us
    pallas_call x1, Pallas kernels, local(): pl.pallas_call(code_body, name='code_grad', grid=(tiles,), out_shape=(jax...  5.17 us

profile of v2, /device:TPU:0, one launch (start us, length us, event | category | flops | bytes accessed | tf_op | source)
XLA Modules:
  0.0 49.5 jit_solution(10381989096318269749)
XLA Ops:
  0.6 43.7 %link_step.1 = (f32[1,64]{1,0:T(1,128)}, bf16[1024,512]{1,0:T(8,128)(2,1)}, bf16[512,1024]{1,0:T(8,128)(2,1)}, bf16[8,32,128]{2,1,0:T(8,128)(2,1)}) custom-call(bf16[1024,1024]{1,0:T(8,128)(2,1)} %bitcast.4, bf16[64,1024]{1,0:T(8,128)(2,1)} %hidden_ref.1, bf16[1024,1024]{1,0:T(8,128)(2,1)} %proj_ref.1, s32[1,64]{1,0:T(1,128)} %bitcast.5), custom_call_target="tpu_custom_call" | custom-call | tf_op jit(solution)/shard_map/link_step/pallas_call | solution.py:281
  44.3 5.2 %code_grad.1 = (f32[1024,1024]{1,0:T(8,128)}, f32[1,64]{1,0:T(1,128)}, f32[32,1024]{1,0:T(8,128)}) custom-call(bf16[1024,512]{1,0:T(8,128)(2,1)} %get-tuple-element.10.gradt_ref, bf16[512,1024]{1,0:T(8,128)(2,1)} %get-tuple-element.11.embed_ref, f32[1,64]{1,0:T(1,128)} %get-tuple-element.12.loss_ref, bf16[8,32,128]{2,1,0:T(8,128)(2,1)} %get-tuple-element.13.parts_ref), custom_call_target="tpu_custom_call" | custom-call | tf_op jit(solution)/shard_map/code_grad/pallas_call | solution.py:324

commit v3 on v2

--- a/solution.py
+++ b/solution.py
@@ -23,10 +23,10 @@
 def body(
     ring, groups, ctx, per,
     codes_ref, hidden_ref, proj_ref, gold_ref,
-    loss_ref, gradt_ref, embed_ref, q_in,
-    codes, proj, perm, rows, held, embed, logits, slopes, scores, grads, gradt, hidt,
+    loss_ref, code_ref, q_in,
+    codes, proj, perm, rows, held, embed, logits, slopes, scores, grads, gradt, hidt, code_low,
     e_own, e_sib, e_sum, e_in, p_own, p_in, q_own,
-    local_sem, h_send, h_recv, hs_send, hs_recv, es_send, es_recv,
+    local_sem, h_send, h_recv, hs_send, hs_recv, es0_send, es0_recv, es_send, es_recv,
     ef_send, ef_recv, z_send, z_recv, q_send, q_recv,
 ):
     width = hidden_ref.shape[1]
@@ -91,9 +91,13 @@
 
     get_proj.wait()
 
-    def forward(owners):
-        count = len(owners) * batch
-        spots = [pl.ds(pl.multiple_of(o * batch, batch), batch) for o in owners]
+    shared = []
+
+    def spots_of(owners):
+        return [pl.ds(pl.multiple_of(o * batch, batch), batch) for o in owners]
+
+    def project(owners):
+        spots = spots_of(owners)
 
         @pl.loop(0, width // tile)
         def _(t):
@@ -101,6 +105,15 @@
             part = dot(jnp.concatenate([held[o] for o in owners], axis=0), proj[:, cols])
             for j, spot in enumerate(spots):
                 embed[spot, cols] = part[j * batch:(j + 1) * batch].astype(BF16)
+
+        for spot in spots:
+            k = len(shared)
+            shared.append(send(embed.at[spot], embed.at[spot], es0_send.at[k], es0_recv.at[k],
+                               {"loop": sibling}))
+
+    def forward(owners):
+        count = len(owners) * batch
+        spots = spots_of(owners)
 
         @pl.loop(0, n_rows // tile)
         def _(t):
@@ -140,7 +153,8 @@
                 for i, (w, x) in enumerate(zip(weights, parts)):
                     slopes[at, i * LANES:(i + 1) * LANES] = (w * scaled) * (x + rest)
 
-    near[0].wait_recv()
+    project([me])
+    shared[0].wait_recv()
     forward([me, sibling])
     mine, theirs = [], []
     for k in range(chips - 1):
@@ -150,12 +164,11 @@
                          hs_recv.at[k], {"loop": sibling}))
         mine.append(src * 2 + par)
         theirs.append(src * 2 + 1 - par)
+    project(mine)
     forward(mine)
-    for copy in near[1:]:
+    for copy in shared[1:]:
         copy.wait_recv()
     forward(theirs)
-    put_embed = pltpu.make_async_copy(embed, embed_ref, local_sem.at[3])
-    put_embed.start()
 
     all_scores = scores[...]
     top_score = jnp.max(all_scores, axis=0, keepdims=True)
@@ -215,8 +228,8 @@
         gradt[:, cols] = lax.dot_general(
             perm[...], grads[cols, :], NT, preferred_element_type=F32).astype(BF16)
 
-    put_gradt = pltpu.make_async_copy(gradt, gradt_ref, local_sem.at[4])
-    put_gradt.start()
+    for copy in near:
+        copy.wait_recv()
     hid_all = held.reshape(2 * half, width)
 
     @pl.loop(0, width // LANES)
@@ -238,6 +251,13 @@
     for k in range(groups - 1):
         to = (group + 1 + k) % groups
         z_far.append(send(p_own.at[to], p_in.at[k], z_send.at[k], z_recv.at[k], {"dp": to}))
+    @pl.loop(0, n_rows // tile)
+    def _(t):
+        at = pl.ds(pl.multiple_of(t * tile, tile), tile)
+        code_low[at, :] = dot(gradt[at, :], embed[...]).astype(BF16)
+
+    put_code = pltpu.make_async_copy(code_low, code_ref, local_sem.at[3])
+    put_code.start()
     total = p_own[group].astype(F32)
     for k in range(groups - 1):
         z_far[k].wait_recv()
@@ -250,14 +270,13 @@
     q_in[me] = q_own[me]
     for k in range(ring - 1):
         q_far[k].wait_recv()
-    put_embed.wait()
-    put_gradt.wait()
-    for copy in far + near + sib + e_far + z_far + q_far:
+    put_code.wait()
+    for copy in far + near + shared + sib + e_far + z_far + q_far:
         copy.wait_send()
 
 
-def code_body(gradt_ref, embed_ref, loss_ref, parts_ref, out_ref, loss_out, proj_out):
-    out_ref[...] = dot(gradt_ref[...], embed_ref[...])
+def code_body(code_ref, loss_ref, parts_ref, out_ref, loss_out, proj_out):
+    out_ref[...] = code_ref[...].astype(F32)
 
     @pl.when(pl.program_id(0) == 0)
     def _():
@@ -278,17 +297,16 @@
     vmem = pl.BlockSpec(memory_space=pltpu.VMEM)
     anywhere = pl.BlockSpec(memory_space=pl.ANY)
     dma = pltpu.SemaphoreType.DMA
-    loss, gradt, embed, parts = pl.pallas_call(
+    loss, code_low, parts = pl.pallas_call(
         functools.partial(body, ring, groups, ctx, per),
         name="link_step",
         out_shape=(
             jax.ShapeDtypeStruct((1, ctx), F32),
-            jax.ShapeDtypeStruct((n_rows, cands), BF16),
-            jax.ShapeDtypeStruct((cands, width), BF16),
+            jax.ShapeDtypeStruct((n_rows, width), BF16),
             jax.ShapeDtypeStruct((ring, out_rows, chunk), BF16),
         ),
         in_specs=[anywhere, vmem, anywhere, vmem],
-        out_specs=(vmem, anywhere, anywhere, vmem),
+        out_specs=(vmem, anywhere, vmem),
         scratch_shapes=[
             pltpu.VMEM((n_rows, width), BF16),
             pltpu.VMEM((width, width), BF16),
@@ -302,6 +320,7 @@
             pltpu.VMEM((cands, n_rows), BF16),
             pltpu.VMEM((n_rows, cands), BF16),
             pltpu.VMEM((width, cands), BF16),
+            pltpu.VMEM((n_rows, width), BF16),
             pltpu.VMEM((chips, 2, cands, chunk), BF16),
             pltpu.VMEM((chips, cands, chunk), BF16),
             pltpu.VMEM((chips, cands, chunk), BF16),
@@ -309,8 +328,9 @@
             pltpu.VMEM((groups, ring, out_rows, chunk), BF16),
             pltpu.VMEM((groups - 1, ring, out_rows, chunk), BF16),
             pltpu.VMEM((ring, out_rows, chunk), BF16),
-            dma((5,)),
+            dma((4,)),
             dma((chips - 1,)), dma((chips - 1,)),
+            dma((chips,)), dma((chips,)),
             dma((chips,)), dma((chips,)),
             dma((chips,)), dma((chips,)),
             dma((chips - 1,)), dma((chips - 1,)),
@@ -331,8 +351,7 @@
             jax.ShapeDtypeStruct((out_rows, width), F32),
         ),
         in_specs=[
-            pl.BlockSpec((n_rows // tiles, cands), lambda t: (t, 0)),
-            pl.BlockSpec((cands, width), lambda t: (0, 0)),
+            pl.BlockSpec((n_rows // tiles, width), lambda t: (t, 0)),
             pl.BlockSpec((1, ctx), lambda t: (0, 0)),
             pl.BlockSpec((ring, out_rows, chunk), lambda t: (0, 0, 0)),
         ],
@@ -341,7 +360,7 @@
             pl.BlockSpec((1, ctx), lambda t: (0, 0)),
             pl.BlockSpec((out_rows, width), lambda t: (0, 0)),
         ),
-    )(gradt, embed, loss, parts)
+    )(code_low, loss, parts)
     return loss.reshape(ctx), code_grad.reshape(ctx, per, width), proj_grad
 
 

time: 49.7 us -> 47.7 us (0.960)
  Pallas kernels: 48.9 us -> 46.9 us
    pallas_call x1, Pallas kernels: 43.7 us -> 42.6 us  [local(): pl.pallas_call(functools.partial(body, ring, groups, ctx, per), name='lin...]
    pallas_call x1, Pallas kernels: 5.17 us -> 4.26 us  [local(): pl.pallas_call(code_body, name='code_grad', grid=(tiles,), out_shape=(jax...]
where the time goes in v3:
time: 47.7 us; the launch traced here: 47.5 us
  Pallas kernels  46.9 us (98%)
  between operations  0.64 us (1%)
    pallas_call x1, Pallas kernels, local(): pl.pallas_call(functools.partial(body, ring, groups, ctx, per), name='lin...  42.6 us
    pallas_call x1, Pallas kernels, local(): pl.pallas_call(code_body, name='code_grad', grid=(tiles,), out_shape=(jax...  4.26 us

profile of v3, /device:TPU:0, one launch (start us, length us, event | category | flops | bytes accessed | tf_op | source)
XLA Modules:
  0.0 47.5 jit_solution(14356154260695755401)
XLA Ops:
  0.6 42.6 %link_step.1 = (f32[1,64]{1,0:T(1,128)}, bf16[1024,1024]{1,0:T(8,128)(2,1)}, bf16[8,32,128]{2,1,0:T(8,128)(2,1)}) custom-call(bf16[1024,1024]{1,0:T(8,128)(2,1)} %bitcast.4, bf16[64,1024]{1,0:T(8,128)(2,1)} %hidden_ref.1, bf16[1024,1024]{1,0:T(8,128)(2,1)} %proj_ref.1, s32[1,64]{1,0:T(1,128)} %bitcast.5), custom_call_target="tpu_custom_call" | custom-call | tf_op jit(solution)/shard_map/link_step/pallas_call | solution.py:300
  43.3 4.3 %code_grad.1 = (f32[1024,1024]{1,0:T(8,128)}, f32[1,64]{1,0:T(1,128)}, f32[32,1024]{1,0:T(8,128)}) custom-call(bf16[1024,1024]{1,0:T(8,128)(2,1)} %get-tuple-element.9.code_ref, f32[1,64]{1,0:T(1,128)} %get-tuple-element.10.loss_ref, bf16[8,32,128]{2,1,0:T(8,128)(2,1)} %get-tuple-element.11.parts_ref), custom_call_target="tpu_custom_call" | custom-call | tf_op jit(solution)/shard_map/code_grad/pallas_call | solution.py:344

commit v4 on v3

--- a/solution.py
+++ b/solution.py
@@ -11,7 +11,7 @@
 F32 = jnp.float32
 BF16 = jnp.bfloat16
 LANES = 128
-STEP = 32
+STEP = 64
 LAG = 1
 NT = (((1,), (1,)), ((), ()))
 
@@ -340,7 +340,7 @@
         compiler_params=pltpu.CompilerParams(
             collective_id=0, has_side_effects=True, vmem_limit_bytes=56 * 2**20),
     )(codes.reshape(n_rows, width), cand_hidden, proj, gold.reshape(1, ctx))
-    tiles = 4
+    tiles = 2
     code_grad, loss, proj_grad = pl.pallas_call(
         code_body,
         name="code_grad",

time: 47.7 us -> 45.4 us (0.952)
  Pallas kernels: 46.9 us -> 44.6 us
    pallas_call x1, Pallas kernels: 42.6 us -> 41.1 us  [local(): pl.pallas_call(functools.partial(body, ring, groups, ctx, per), name='lin...]
    pallas_call x1, Pallas kernels: 4.26 us -> 3.43 us  [local(): pl.pallas_call(code_body, name='code_grad', grid=(tiles,), out_shape=(jax...]
where the time goes in v4:
time: 45.4 us; the launch traced here: 45.2 us
  Pallas kernels  44.6 us (98%)
  between operations  0.64 us (1%)
    pallas_call x1, Pallas kernels, local(): pl.pallas_call(functools.partial(body, ring, groups, ctx, per), name='lin...  41.1 us
    pallas_call x1, Pallas kernels, local(): pl.pallas_call(code_body, name='code_grad', grid=(tiles,), out_shape=(jax...  3.43 us

profile of v4, /device:TPU:0, one launch (start us, length us, event | category | flops | bytes accessed | tf_op | source)
XLA Modules:
  0.0 45.2 jit_solution(5744120243373119581)
XLA Ops:
  0.6 41.1 %link_step.1 = (f32[1,64]{1,0:T(1,128)}, bf16[1024,1024]{1,0:T(8,128)(2,1)}, bf16[8,32,128]{2,1,0:T(8,128)(2,1)}) custom-call(bf16[1024,1024]{1,0:T(8,128)(2,1)} %bitcast.4, bf16[64,1024]{1,0:T(8,128)(2,1)} %hidden_ref.1, bf16[1024,1024]{1,0:T(8,128)(2,1)} %proj_ref.1, s32[1,64]{1,0:T(1,128)} %bitcast.5), custom_call_target="tpu_custom_call" | custom-call | tf_op jit(solution)/shard_map/link_step/pallas_call | solution.py:300
  41.8 3.4 %code_grad.1 = (f32[1024,1024]{1,0:T(8,128)}, f32[1,64]{1,0:T(1,128)}, f32[32,1024]{1,0:T(8,128)}) custom-call(bf16[1024,1024]{1,0:T(8,128)(2,1)} %get-tuple-element.9.code_ref, f32[1,64]{1,0:T(1,128)} %get-tuple-element.10.loss_ref, bf16[8,32,128]{2,1,0:T(8,128)(2,1)} %get-tuple-element.11.parts_ref), custom_call_target="tpu_custom_call" | custom-call | tf_op jit(solution)/shard_map/code_grad/pallas_call | solution.py:344
